TPU v7x, 256 devices: a whole 4x4x8 slice. The times are simulated.
256 devices in a mesh: tmpl: 8 (over z), dp: 8 (over y, core), mp: 4 (over x).
Axes of the slice: x: 4, y: 4, z: 8, core: 2. Of those that a mesh axis runs over, the one named last changes fastest.
Arguments:
- hidden: bfloat16 [8, 32, 8, 8192], P('tmpl', ('dp', 'mp')), as said below
- norm_gain: float32 [8192], replicated, may hold values from 0.5 to 1.5
- head_weight: bfloat16 [152064, 8192], P(('tmpl', 'dp', 'mp'))
- lengths: int32 [32, 4], P(('dp', 'mp')), may hold values from 1 to 2, as said below
- targets: int32 [32, 4, 2], P(('dp', 'mp')), may hold values from 0 to 152063
- destinations: int32 [32, 4], P(('dp', 'mp')), may hold values from 0 to 7, as said below
Outputs:
- packed_logprobs: float32 [1536], P(('tmpl', 'dp', 'mp'))
- row_loglik: float32 [8, 32, 4], P('tmpl', ('dp', 'mp'))
- scores: float32 [32, 4], P(('dp', 'mp'))
Inputs may be any that keep to these rules, and one draw needn't show every extreme that they name: `lengths`: lengths and destinations hold for every template. For each index of mp and each destination j, the rows with destination j on the devices of that mp index hold exactly 6 tokens together; some row has 2 tokens. `destinations`: A device has at most 1 row with the same destination, and exactly 1 with some destination. `hidden`: slots beyond a row's length are read by no output.
All inputs are finite; a program needn't handle non-finite values.
Results may differ from a plain program's by a relative error of at most 0.0003.
Values may be sent and summed in bfloat16 or wider, within the bound.
No kernel may reach another device: no remote copies, remote signals or barrier semaphores. Data moves between devices by JAX's collectives and lax.ppermute only.
A program may use at most 192 MiB of HBM per device.

v0:
```python
import math
import jax
import jax.numpy as jnp
from jax import lax
from jax.sharding import Mesh
from jax.sharding import PartitionSpec as P

DP = ("dp_0", "dp_1")
TMPL_DP_MP = ("tmpl", "dp_0", "dp_1", "mp")
TMPL_DP = ("tmpl", "dp_0", "dp_1")
DP_MP = ("dp_0", "dp_1", "mp")


def side_by_side(arrays, axis, split_dim, concat_dim, along):
    ends, at = ([], 0)
    for a in arrays[:-1]:
        at += a.shape[along]
        ends.append(at)
    both = jnp.concatenate(arrays, axis=along)
    return tuple(
        jnp.split(
            lax.all_to_all(both, axis, split_axis=split_dim, concat_axis=concat_dim, tiled=True),
            ends,
            axis=along,
        )
    )


def in_order(parts, dim):
    shape = list(parts.shape[1:])
    shape[dim] *= parts.shape[0]
    return jnp.moveaxis(parts, 0, dim).reshape(shape)


def sent_to_all(value, axis):
    copies = jnp.broadcast_to(value, (lax.axis_size(axis), *value.shape))
    return lax.all_to_all(copies, axis, split_axis=0, concat_axis=0, tiled=True)


def gathered_copies(value, axis, dim):
    return in_order(sent_to_all(value, axis), dim)


def all_in_one(value, axis):
    leaves = jax.tree.leaves(value)
    order = sorted(range(len(leaves)), key=lambda k: -leaves[k].size)
    width = (1, *leaves[order[0]].shape)[-1]
    lines = [
        jnp.pad(leaves[k].reshape(-1), (0, -leaves[k].size % width)).reshape(-1, width)
        for k in order
    ]
    both, at, found = (lax.all_gather(jnp.concatenate(lines), axis), 0, {})
    for k, line in zip(order, lines):
        slab = both[:, at : at + len(line)].reshape(len(both), -1)
        found[k] = slab[:, : leaves[k].size].reshape(-1, *leaves[k].shape)
        at += len(line)
    numbers = iter(range(len(leaves)))
    return jax.tree.map(lambda _: found[next(numbers)], value)


def combined_by_axis(value, axes, combine):
    for axis in axes:
        pieces = all_in_one(value, axis)
        value = jax.tree.map(lambda part: part[0], pieces)
        for k in range(1, lax.axis_size(axis)):
            value = combine(value, jax.tree.map(lambda part: part[k], pieces))
    return value


def all_in_one_2(value, axis):
    leaves = jax.tree.leaves(value)
    order = sorted(range(len(leaves)), key=lambda k: -leaves[k].size)
    width = (1, *leaves[order[0]].shape)[-1]
    lines = [
        jnp.pad(leaves[k].reshape(-1), (0, -leaves[k].size % width)).reshape(-1, width)
        for k in order
    ]
    both, at, found = (sent_to_all(jnp.concatenate(lines), axis), 0, {})
    for k, line in zip(order, lines):
        slab = both[:, at : at + len(line)].reshape(len(both), -1)
        found[k] = slab[:, : leaves[k].size].reshape(-1, *leaves[k].shape)
        at += len(line)
    numbers = iter(range(len(leaves)))
    return jax.tree.map(lambda _: found[next(numbers)], value)


def collected_alike(value, axis):
    leaves, found = (jax.tree.leaves(value), {})
    for first, a in enumerate(leaves):
        if first not in found:
            alike = [k for k, b in enumerate(leaves) if b.dtype == a.dtype]
            got = (
                all_in_one_2([leaves[k] for k in alike], axis)
                if len(alike) > 1
                else [sent_to_all(a, axis)]
            )
            for k, b in zip(alike, got):
                found[k] = b
    numbers = iter(range(len(leaves)))
    return jax.tree.map(lambda _: found[next(numbers)], value)


def joined_by_halves(pieces, combine):
    while len(jax.tree.leaves(pieces)[0]) > 1:
        pieces = jax.vmap(combine)(
            *(jax.tree.map(lambda part: part[side::2], pieces) for side in (0, 1))
        )
    return jax.tree.map(lambda part: part[0], pieces)


def joined_all(value, axis, combine):
    pieces = collected_alike(value, axis)
    return joined_by_halves(pieces, combine)


def join_stats(first, second):
    highest = jnp.maximum(first[0], second[0])
    summed = first[1] * jnp.exp(first[0] - highest) + second[1] * jnp.exp(second[0] - highest)
    return (highest, summed, first[2] + second[2])


def join_templates(first, second):
    highest = jnp.maximum(first[0], second[0])
    summed = first[1] * jnp.exp(first[0] - highest) + second[1] * jnp.exp(second[0] - highest)
    return (highest, summed)


def on_device(hidden, norm_gain, head_weight, lengths, targets, destinations):
    width = hidden.shape[-1]
    row_count = lengths.shape[0] * lengths.shape[1]
    span_len = targets.shape[-1]
    dp_count = lax.axis_size(DP)
    pair_rows = max(1, row_count // dp_count)
    capacity = row_count * 3 // 2
    slot_count = pair_rows * span_len
    tokens = hidden.reshape(row_count * span_len, width).astype(jnp.float32)
    meansq = jnp.mean(tokens * tokens, axis=1, keepdims=True)
    normed = (tokens * lax.rsqrt(meansq + 1e-06) * norm_gain).astype(jnp.bfloat16)
    row_len = lengths.reshape(row_count)
    row_dest = destinations.reshape(row_count)
    token_target = targets.reshape(row_count * span_len)
    position = jnp.arange(span_len, dtype=jnp.int32)
    live = (position[None, :] < row_len[:, None]).reshape(-1)
    dest_hot = (row_dest[:, None] == jnp.arange(dp_count, dtype=jnp.int32)[None, :]).astype(
        jnp.int32
    )
    earlier = jnp.cumsum(dest_hot, axis=0) - dest_hot
    row_rank = jnp.sum(earlier * dest_hot, axis=1)
    token_slot = (
        (row_dest * slot_count + row_rank * span_len)[:, None] + position[None, :]
    ).reshape(-1)
    send_hot = (
        jnp.arange(dp_count * slot_count, dtype=jnp.int32)[:, None] == token_slot[None, :]
    ) & live[None, :]
    send_rows = jnp.dot(
        send_hot.astype(jnp.bfloat16), normed, preferred_element_type=jnp.float32
    ).astype(jnp.bfloat16)
    send_rows = send_rows.reshape(dp_count, slot_count, width)
    send_target = jnp.sum(jnp.where(send_hot, token_target[None, :], 0), axis=1).reshape(
        dp_count, slot_count
    )
    row_slot = row_dest * pair_rows + row_rank
    send_len = jnp.sum(
        jnp.where(
            jnp.arange(dp_count * pair_rows, dtype=jnp.int32)[:, None] == row_slot[None, :],
            row_len[None, :],
            0,
        ),
        axis=1,
    )
    send_len = send_len.reshape(dp_count, pair_rows)
    got_rows, got_target, got_len = (
        lax.all_to_all(send_rows, DP, split_axis=0, concat_axis=0, tiled=True),
        *side_by_side((send_target, send_len), DP, 0, 0, 1),
    )
    flat_len = got_len.reshape(-1)
    row_start = jnp.cumsum(flat_len) - flat_len
    place = (row_start[:, None] + position[None, :]).reshape(-1)
    used = (position[None, :] < flat_len[:, None]).reshape(-1)
    keep_hot = (jnp.arange(capacity, dtype=jnp.int32)[:, None] == place[None, :]) & used[None, :]
    balanced = jnp.dot(
        keep_hot.astype(jnp.bfloat16),
        got_rows.reshape(-1, width),
        preferred_element_type=jnp.float32,
    ).astype(jnp.bfloat16)
    balanced_target = jnp.sum(jnp.where(keep_hot, got_target.reshape(-1)[None, :], 0), axis=1)
    my_index = lax.axis_index(TMPL_DP_MP)
    vocab_ids = my_index * head_weight.shape[0] + jnp.arange(head_weight.shape[0], dtype=jnp.int32)
    near_rows, near_target = (
        gathered_copies(balanced, "mp", 0),
        gathered_copies(balanced_target, "mp", 0),
    )
    every_rows, every_target = (
        lax.all_gather(near_rows, TMPL_DP, axis=0, tiled=True),
        lax.all_gather(near_target, TMPL_DP, axis=0, tiled=True),
    )
    logits = lax.dot_general(
        every_rows, head_weight, (((1,), (1,)), ((), ())), preferred_element_type=jnp.float32
    )
    row_high = jnp.max(logits, axis=1)
    row_summed = jnp.sum(jnp.exp(logits - row_high[:, None]), axis=1)
    picked = jnp.sum(jnp.where(vocab_ids[None, :] == every_target[:, None], logits, 0.0), axis=1)
    own_start = my_index * capacity
    merged = combined_by_axis((row_high, row_summed, picked), TMPL_DP_MP, join_stats)
    own_high = lax.dynamic_slice_in_dim(merged[0], own_start, capacity)
    own_summed = lax.dynamic_slice_in_dim(merged[1], own_start, capacity)
    own_picked = lax.dynamic_slice_in_dim(merged[2], own_start, capacity)
    token_logprob = own_picked - own_high - jnp.log(own_summed)
    back_vals = jnp.sum(jnp.where(keep_hot, token_logprob[:, None], 0.0), axis=0).reshape(
        dp_count, slot_count
    )
    returned = lax.all_to_all(back_vals, DP, split_axis=0, concat_axis=0, tiled=True)
    token_vals = jnp.sum(jnp.where(send_hot, returned.reshape(-1)[:, None], 0.0), axis=0)
    row_loglik = jnp.sum(token_vals.reshape(row_count, span_len), axis=1)
    highest, summed = joined_all((row_loglik, jnp.ones_like(row_loglik)), "tmpl", join_templates)
    scores = highest + jnp.log(summed) - math.log(lax.axis_size("tmpl"))
    return (token_logprob, row_loglik.reshape((1,) + lengths.shape), scores.reshape(lengths.shape))


def solution(mesh):
    torus = Mesh(
        mesh.devices.reshape(mesh.shape["tmpl"], 4, 2, mesh.shape["mp"]),
        ("tmpl", "dp_0", "dp_1", "mp"),
    )
    in_specs = (
        P("tmpl", DP_MP, None, None),
        P(),
        P(TMPL_DP_MP, None),
        P(DP_MP, None),
        P(DP_MP, None, None),
        P(DP_MP, None),
    )
    out_specs = (P(TMPL_DP_MP), P("tmpl", DP_MP, None), P(DP_MP, None))
    return jax.shard_map(
        on_device, mesh=torus, in_specs=in_specs, out_specs=out_specs, check_vma=False
    )
```

profile of v0, /device:TPU:2, one launch (start us, length us, event | category | flops | bytes accessed | tf_op | source)
XLA Modules:
  0.0 272.0 jit_solution(1676549541065805954)
XLA Ops:
  7.2 0.7 fusion.62
  7.9 0.8 select_reduce_fusion.6
  8.8 0.7 add_multiply_fusion
  9.4 0.7 fusion.77
  10.3 0.7 iota_compare_fusion.4
  11.1 0.7 select_reduce_fusion.5
  11.9 0.8 copy.29
  12.9 0.7 pad_add_fusion
  13.6 4.5 %all-to-all-start = ((s32[8,1,3]{2,1,0:T(1,128)}), s32[8,1,3]{2,1,0:T(1,128)S(1)}, u32[]{:S(2)}, u32[]{:S(2)}) async-start(s32[8,1,3]{2,1,0:T(1,128)} %bitcast.53), calls=%async_computation | async-start | bytes 8192 | tf_op jit(solution)/shard_map/all_to_all | solution.py:22
  18.1 1.1 fusion
  19.2 1.3 convolution_convert_fusion
  20.4 0.9 reshape.1033
  21.3 2.1 all-to-all-done
  23.4 3.4 %all-to-all-start.1 = ((bf16[8,2,8192]{2,1,0:T(2,128)(2,1)}), bf16[8,2,8192]{2,1,0:T(2,128)(2,1)S(1)}, u32[]{:S(2)}, u32[]{:S(2)}) async-start(bf16[8,2,8192]{2,1,0:T(2,128)(2,1)} %reshape.1033), calls=%async_computation.1 | async-start | bytes 524288 | tf_op jit(solution)/shard_map/all_to_all | solution.py:173
  27.4 6.8 %all-to-all-done.1 = bf16[8,2,8192]{2,1,0:T(2,128)(2,1)S(1)} async-done(((bf16[8,2,8192]{2,1,0:T(2,128)(2,1)}), bf16[8,2,8192]{2,1,0:T(2,128)(2,1)S(1)}, u32[]{:S(2)}, u32[]{:S(2)}) %all-to-all-start.1) | async-done | bytes 262176 | tf_op jit(solution)/shard_map/all_to_all | solution.py:173
  34.5 12.3 %all_to_all.42 = bf16[4,6,8192]{2,1,0:T(8,128)(2,1)S(1)} all-to-all(bf16[4,6,8192]{2,1,0:T(8,128)(2,1)S(1)} %broadcast_in_dim.101), channel_id=1, replica_groups=mesh['tmpl'=8,'dp_0'=4,'dp_1'=2,'mp'=4] {'mp'}, dimensions={0} | all-to-all | bytes 786432 | tf_op jit(solution)/shard_map/all_to_all | solution.py:37
  46.8 0.9 reshape.1035
  49.9 4.6 %all-to-all-start.3 = ((s32[4,1,6]{2,1,0:T(1,128)}), s32[4,1,6]{2,1,0:T(1,128)S(1)}, u32[]{:S(2)}, u32[]{:S(2)}) async-start(s32[4,1,6]{2,1,0:T(1,128)} %broadcast_in_dim.105), calls=%async_computation.3 | async-start | bytes 4096 | tf_op jit(solution)/shard_map/all_to_all | solution.py:37
  54.5 3.8 %all-to-all-done.3 = s32[4,1,6]{2,1,0:T(1,128)S(1)} async-done(((s32[4,1,6]{2,1,0:T(1,128)}), s32[4,1,6]{2,1,0:T(1,128)S(1)}, u32[]{:S(2)}, u32[]{:S(2)}) %all-to-all-start.3) | async-done | bytes 128 | tf_op jit(solution)/shard_map/all_to_all | solution.py:37
  58.9 0.7 reduce.22
  59.9 22.7 %all-reduce.1 = s32[1536]{0:T(1024)S(1)} all-reduce(s32[1536]{0:T(1024)S(1)} %dynamic-update-slice), channel_id=1, replica_groups=mesh['tmpl'=8,'dp_0'=4,'dp_1'=2,'mp'=4] {'tmpl','dp_0','dp_1'}, use_global_device_ids=true, to_apply=%add.1 | all-reduce | flops 1536 | bytes 12288
  82.6 86.2 %all-gather.10.cloned.1.call-done = bf16[1536,8192]{1,0:T(8,128)(2,1)} async-done(((bf16[24,8192]{1,0:T(8,128)(2,1)}), bf16[1536,8192]{1,0:T(8,128)(2,1)}) %all-gather.10.cloned.1.call-update) | async-done | bytes 25165840 | tf_op jit(solution)/shard_map/all_gather | solution.py:194
  168.7 21.1 %fusion.84 = (f32[1536]{0:T(1024)S(1)}, f32[1536,594]{0,1:T(8,128)S(1)}) fusion(bf16[1536,8192]{1,0:T(8,128)(2,1)} %all-gather.10.cloned.1.call-done, bf16[594,8192]{1,0:T(8,128)(2,1)} %param.8), kind=kOutput, calls=%fused_computation.174 | convolution fusion | flops 14949410816 | bytes 38553600 | tf_op jit(solution)/shard_map/dot_general | solution.py:197
  189.9 0.9 exponential_reduce_fusion
  190.8 24.7 %all-gather.4 = f32[8,3,1536]{2,1,0:T(4,128)S(1)} all-gather(f32[1,3,1536]{2,1,0:T(4,128)S(1)} %maximum_bitcast_fusion), channel_id=2, replica_groups=mesh['tmpl'=8,'dp_0'=4,'dp_1'=2,'mp'=4] {'tmpl'}, dimensions={0}, use_global_device_ids=true | all-gather | bytes 165888 | tf_op jit(solution)/shard_map/all_gather | solution.py:52
  215.7 11.9 %all-gather.5 = f32[4,3,1536]{2,1,0:T(4,128)S(1)} all-gather(f32[1,3,1536]{2,1,0:T(4,128)S(1)} %maximum_bitcast_fusion.1), channel_id=3, replica_groups=mesh['tmpl'=8,'dp_0'=4,'dp_1'=2,'mp'=4] {'dp_0'}, dimensions={0}, use_global_device_ids=true | all-gather | bytes 92160 | tf_op jit(solution)/shard_map/all_gather | solution.py:52
  227.8 1.8 all-gather.6
  229.7 11.9 %all-gather.7 = f32[4,3,1536]{2,1,0:T(4,128)S(1)} all-gather(f32[1,3,1536]{2,1,0:T(4,128)S(1)} %maximum_bitcast_fusion.3), channel_id=5, replica_groups=mesh['tmpl'=8,'dp_0'=4,'dp_1'=2,'mp'=4] {'mp'}, dimensions={0}, use_global_device_ids=true | all-gather | bytes 92160 | tf_op jit(solution)/shard_map/all_gather | solution.py:52
  242.1 7.8 %all_to_all.43 = f32[8,1,2]{2,1,0:T(1,128)S(1)} all-to-all(f32[8,1,2]{2,1,0:T(1,128)S(1)} %bitcast.310), channel_id=1, replica_groups=mesh['tmpl'=8,'dp_0'=4,'dp_1'=2,'mp'=4] {'dp_0','dp_1'}, dimensions={0} | all-to-all | bytes 128 | tf_op jit(solution)/shard_map/all_to_all | solution.py:212
  250.4 0.7 reduce.23
  251.6 11.8 %all_to_all.44 = f32[8,2,4]{2,1,0:T(2,128)S(1)} all-to-all(f32[8,2,4]{2,1,0:T(2,128)S(1)} %broadcast_in_dim.112), channel_id=1, replica_groups=mesh['tmpl'=8,'dp_0'=4,'dp_1'=2,'mp'=4] {'tmpl'}, dimensions={0} | all-to-all | bytes 512 | tf_op jit(solution)/shard_map/all_to_all | solution.py:37
  264.5 0.6 copy.38
  (79 shorter events, 6.8 us)
Async XLA Ops:
  7.2 40.6 %copy-start.2 = (u32[256]{0:T(256)S(1)}, u32[256]{0:T(256)}, u32[]{:S(2)}) copy-start(u32[256]{0:T(256)} %constant.64) | copy-start | bytes 3076
  13.6 9.8 %all-to-all-start = ((s32[8,1,3]{2,1,0:T(1,128)}), s32[8,1,3]{2,1,0:T(1,128)S(1)}, u32[]{:S(2)}, u32[]{:S(2)}) async-start(s32[8,1,3]{2,1,0:T(1,128)} %bitcast.53), calls=%async_computation | async-start | bytes 8192 | tf_op jit(solution)/shard_map/all_to_all | solution.py:22
  23.4 10.8 %all-to-all-start.1 = ((bf16[8,2,8192]{2,1,0:T(2,128)(2,1)}), bf16[8,2,8192]{2,1,0:T(2,128)(2,1)S(1)}, u32[]{:S(2)}, u32[]{:S(2)}) async-start(bf16[8,2,8192]{2,1,0:T(2,128)(2,1)} %reshape.1033), calls=%async_computation.1 | async-start | bytes 524288 | tf_op jit(solution)/shard_map/all_to_all | solution.py:173
  26.8 141.9 %all-gather.10.cloned.1.call-start = ((), (), s32[]{:S(2)}) async-start(), calls=%async_computation.6 | async-start | bytes 25559040 | tf_op jit(solution)/shard_map/all_gather | solution.py:194
  49.9 8.4 %all-to-all-start.3 = ((s32[4,1,6]{2,1,0:T(1,128)}), s32[4,1,6]{2,1,0:T(1,128)S(1)}, u32[]{:S(2)}, u32[]{:S(2)}) async-start(s32[4,1,6]{2,1,0:T(1,128)} %broadcast_in_dim.105), calls=%async_computation.3 | async-start | bytes 4096 | tf_op jit(solution)/shard_map/all_to_all | solution.py:37
  241.9 23.2 %copy-start = (f32[6]{0:T(128)}, f32[6]{0:T(128)S(1)}, u32[]{:S(2)}) copy-start(f32[6]{0:T(128)S(1)} %fusion.76) | copy-start | bytes 76
  251.6 13.6 %copy-start.1 = (f32[4]{0:T(128)}, f32[4]{0:T(128)S(1)}, u32[]{:S(2)}) copy-start(f32[4]{0:T(128)S(1)} %reduce_sum.102) | copy-start | bytes 52
Sparse Core Ops, SparseCore 0:
  47.9 120.7 all-gather.9
where the time goes:
time: 273 us; the launch traced here: 272 us
  blocking collectives  105 us (38%)
  waiting for transfers between devices  98.9 us (36%)
  matrix products  22.5 us (8%)
  between operations  15 us (5%)
  starting transfers between devices  12.5 us (5%)
  other arithmetic  10 us (4%)
  local copies, waits for them, and re-layouts  8.07 us (3%)
    all_gather x1, waiting for transfers between devices, on_device(): lax.all_gather(near_rows, TMPL_DP, axis=0, tiled=True)  86.2 us
    all_gather x4, blocking collectives, all_in_one(): both, at, found = (lax.all_gather(jnp.concatenate(lines), axis), 0, {})  50.4 us
    all_to_all x2, blocking collectives, sent_to_all(): return lax.all_to_all(copies, axis, split_axis=0, concat_axis=0, tiled=True)  24.1 us
    unnamed x1, blocking collectives  22.7 us
    dot_general x1, matrix products, on_device(): lax.dot_general(every_rows, head_weight, (((1,), (1,)), ((), ())), prefer...  21.1 us
    all_to_all x1, blocking collectives, on_device(): lax.all_to_all(back_vals, DP, split_axis=0, concat_axis=0, tiled=True)  7.82 us
    all_to_all x1, waiting for transfers between devices, on_device(): lax.all_to_all(send_rows, DP, split_axis=0, concat_axis=0, tiled=True)  6.78 us
  transfers between devices with their start and end apart: 4, of which 4 were waited for; matrix products, arithmetic and copies ran while one was open for 2% of the time, Pallas kernels for 0%

commit v1 on v0

--- a/solution.py
+++ b/solution.py
@@ -1,3 +1,4 @@
+import functools
 import math
 import jax
 import jax.numpy as jnp
@@ -9,6 +10,21 @@
 TMPL_DP_MP = ("tmpl", "dp_0", "dp_1", "mp")
 TMPL_DP = ("tmpl", "dp_0", "dp_1")
 DP_MP = ("dp_0", "dp_1", "mp")
+
+
+def treat_loops(page, chip_axis, out_dim):
+    return jnp.concatenate(
+        lax.all_to_all(
+            jnp.stack(lax.axis_size(chip_axis) * [page]),
+            split_axis=0,
+            axis_name=chip_axis,
+            concat_axis=0,
+        ),
+        axis=out_dim,
+    )
+
+
+_fill_axis_part = functools.partial(treat_loops, chip_axis=TMPL_DP, out_dim=0)
 
 
 def side_by_side(arrays, axis, split_dim, concat_dim, along):
@@ -191,7 +207,7 @@
         gathered_copies(balanced_target, "mp", 0),
     )
     every_rows, every_target = (
-        lax.all_gather(near_rows, TMPL_DP, axis=0, tiled=True),
+        _fill_axis_part(near_rows),
         lax.all_gather(near_target, TMPL_DP, axis=0, tiled=True),
     )
     logits = lax.dot_general(

time: 273 us -> 737 us (2.70)
  blocking collectives: 105 us -> 637 us
  waiting for transfers between devices: 98.9 us -> 19.9 us
  starting transfers between devices: 12.5 us -> 27.8 us
  between operations: 15 us -> 1.55 us
  local copies, waits for them, and re-layouts: 8.07 us -> 16.6 us
    unnamed x1, blocking collectives: 22.7 us -> 562 us
    all_gather x1 -> x0, waiting for transfers between devices: 86.2 us -> none  [on_device(): lax.all_gather(near_rows, TMPL_DP, axis=0, tiled=True)]
    all_to_all x2 -> x1, blocking collectives: 24.1 us -> 12.5 us  [sent_to_all(): return lax.all_to_all(copies, axis, split_axis=0, concat_axis=0, tiled=True)]
    all_to_all x0 -> x1, starting transfers between devices: none -> 10.4 us  [treat_loops(): lax.all_to_all(jnp.stack(lax.axis_size(chip_axis) * [page]), split_axis=0...]
    another operation x0 -> x2, local copies, waits for them, and re-layouts: none -> 8.72 us  [treat_loops(): jnp.stack(lax.axis_size(chip_axis) * [page])]
  transfers between devices with their start and end apart: 4 -> 5, of which waited for: 4 -> 4; matrix products, arithmetic and copies ran while one was open for 2% -> 1% of each run, Pallas kernels for 0% -> 0%
where the time goes in v1:
time: 737 us; the launch traced here: 735 us
  blocking collectives  637 us (86%)
  starting transfers between devices  27.8 us (4%)
  matrix products  22.5 us (3%)
  waiting for transfers between devices  19.9 us (3%)
  local copies, waits for them, and re-layouts  16.6 us (2%)
  other arithmetic  10 us (1%)
    unnamed x1, blocking collectives  562 us
    all_gather x4, blocking collectives, all_in_one(): both, at, found = (lax.all_gather(jnp.concatenate(lines), axis), 0, {})  52.4 us
    dot_general x1, matrix products, on_device(): lax.dot_general(every_rows, head_weight, (((1,), (1,)), ((), ())), prefer...  21.1 us
  transfers between devices with their start and end apart: 5, of which 4 were waited for; matrix products, arithmetic and copies ran while one was open for 1% of the time, Pallas kernels for 0%

profile of v1, /device:TPU:2, one launch (start us, length us, event | category | flops | bytes accessed | tf_op | source)
XLA Modules:
  0.0 735.3 jit_solution(8146623075030684807)
XLA Ops:
  0.6 0.7 fusion.62
  1.4 0.8 select_reduce_fusion.6
  2.2 0.7 add_multiply_fusion
  3.7 0.7 iota_compare_fusion.4
  4.5 0.7 select_reduce_fusion.5
  5.4 0.8 copy.29
  6.4 0.7 pad_add_fusion
  7.0 4.5 all-to-all-start
  11.5 1.1 fusion
  12.6 1.2 convolution_convert_fusion
  13.9 0.9 reshape.1035
  14.7 2.1 all-to-all-done
  16.8 3.4 all-to-all-start.1
  20.8 6.8 all-to-all-done.1
  27.9 0.8 broadcast_in_dim.101
  28.8 4.8 all-to-all-start.2
  33.9 7.4 %all-to-all-done.2 = bf16[4,6,8192]{2,1,0:T(8,128)(2,1)S(1)} async-done(((bf16[4,6,8192]{2,1,0:T(8,128)(2,1)}), bf16[4,6,8192]{2,1,0:T(8,128)(2,1)S(1)}, u32[]{:S(2)}, u32[]{:S(2)}) %all-to-all-start.2) | async-done | bytes 393248 | tf_op jit(solution)/shard_map/all_to_all | solution.py:53
  41.8 4.7 all-to-all-start.4
  46.7 3.7 all-to-all-done.4
  50.3 8.6 %stack.3 = bf16[64,24,8192]{2,1,0:T(8,128)(2,1)} broadcast(bf16[24,8192]{1,0:T(8,128)(2,1)S(1)} %stack_reshape.2), dimensions={1,2} | broadcast | bytes 25559040 | tf_op jit(solution)/shard_map/stack | solution.py:18
  58.9 10.4 %all-to-all-start.3 = ((bf16[64,24,8192]{2,1,0:T(8,128)(2,1)}), bf16[64,24,8192]{2,1,0:T(8,128)(2,1)}, u32[]{:S(2)}, u32[]{:S(2)}) async-start(bf16[64,24,8192]{2,1,0:T(8,128)(2,1)} %stack.3), calls=%async_computation.3 | async-start | bytes 50331648 | tf_op jit(solution)/shard_map/all_to_all | solution.py:17
  71.1 0.7 reduce.22
  72.1 562.3 %all-reduce.1 = s32[1536]{0:T(1024)S(1)} all-reduce(s32[1536]{0:T(1024)S(1)} %dynamic-update-slice), channel_id=1, replica_groups=mesh['tmpl'=8,'dp_0'=4,'dp_1'=2,'mp'=4] {'tmpl','dp_0','dp_1'}, use_global_device_ids=true, to_apply=%add.1 | all-reduce | flops 1536 | bytes 12288
  634.4 21.1 %fusion.84 = (f32[1536]{0:T(1024)S(1)}, f32[1536,594]{0,1:T(8,128)S(1)}) fusion(bf16[1536,8192]{1,0:T(8,128)(2,1)} %bitcast.11, bf16[594,8192]{1,0:T(8,128)(2,1)} %param.8), kind=kOutput, calls=%fused_computation.174 | convolution fusion | flops 14949410816 | bytes 38553600 | tf_op jit(solution)/shard_map/dot_general | solution.py:213
  655.5 0.9 exponential_reduce_fusion
  656.5 26.2 %all-gather.4 = f32[8,3,1536]{2,1,0:T(4,128)S(1)} all-gather(f32[1,3,1536]{2,1,0:T(4,128)S(1)} %maximum_bitcast_fusion), channel_id=2, replica_groups=mesh['tmpl'=8,'dp_0'=4,'dp_1'=2,'mp'=4] {'tmpl'}, dimensions={0}, use_global_device_ids=true | all-gather | bytes 165888 | tf_op jit(solution)/shard_map/all_gather | solution.py:68
  682.9 13.2 %all-gather.5 = f32[4,3,1536]{2,1,0:T(4,128)S(1)} all-gather(f32[1,3,1536]{2,1,0:T(4,128)S(1)} %maximum_bitcast_fusion.1), channel_id=3, replica_groups=mesh['tmpl'=8,'dp_0'=4,'dp_1'=2,'mp'=4] {'dp_0'}, dimensions={0}, use_global_device_ids=true | all-gather | bytes 92160 | tf_op jit(solution)/shard_map/all_gather | solution.py:68
  696.3 1.8 all-gather.6
  698.2 11.2 %all-gather.7 = f32[4,3,1536]{2,1,0:T(4,128)S(1)} all-gather(f32[1,3,1536]{2,1,0:T(4,128)S(1)} %maximum_bitcast_fusion.3), channel_id=5, replica_groups=mesh['tmpl'=8,'dp_0'=4,'dp_1'=2,'mp'=4] {'mp'}, dimensions={0}, use_global_device_ids=true | all-gather | bytes 92160 | tf_op jit(solution)/shard_map/all_gather | solution.py:68
  709.8 9.6 %all_to_all.47 = f32[8,1,2]{2,1,0:T(1,128)S(1)} all-to-all(f32[8,1,2]{2,1,0:T(1,128)S(1)} %bitcast.311), channel_id=1, replica_groups=mesh['tmpl'=8,'dp_0'=4,'dp_1'=2,'mp'=4] {'dp_0','dp_1'}, dimensions={0} | all-to-all | bytes 128 | tf_op jit(solution)/shard_map/all_to_all | solution.py:228
  719.9 0.7 reduce.23
  721.1 12.5 %all_to_all.48 = f32[8,2,4]{2,1,0:T(2,128)S(1)} all-to-all(f32[8,2,4]{2,1,0:T(2,128)S(1)} %broadcast_in_dim.112), channel_id=1, replica_groups=mesh['tmpl'=8,'dp_0'=4,'dp_1'=2,'mp'=4] {'tmpl'}, dimensions={0} | all-to-all | bytes 512 | tf_op jit(solution)/shard_map/all_to_all | solution.py:53
  (80 shorter events, 8.1 us)
Async XLA Ops:
  7.0 9.8 %all-to-all-start = ((s32[8,1,3]{2,1,0:T(1,128)}), s32[8,1,3]{2,1,0:T(1,128)S(1)}, u32[]{:S(2)}, u32[]{:S(2)}) async-start(s32[8,1,3]{2,1,0:T(1,128)} %bitcast.54), calls=%async_computation | async-start | bytes 8192 | tf_op jit(solution)/shard_map/all_to_all | solution.py:38
  16.8 10.8 %all-to-all-start.1 = ((bf16[8,2,8192]{2,1,0:T(2,128)(2,1)}), bf16[8,2,8192]{2,1,0:T(2,128)(2,1)S(1)}, u32[]{:S(2)}, u32[]{:S(2)}) async-start(bf16[8,2,8192]{2,1,0:T(2,128)(2,1)} %reshape.1035), calls=%async_computation.1 | async-start | bytes 524288 | tf_op jit(solution)/shard_map/all_to_all | solution.py:189
  28.8 12.5 %all-to-all-start.2 = ((bf16[4,6,8192]{2,1,0:T(8,128)(2,1)}), bf16[4,6,8192]{2,1,0:T(8,128)(2,1)S(1)}, u32[]{:S(2)}, u32[]{:S(2)}) async-start(bf16[4,6,8192]{2,1,0:T(8,128)(2,1)} %broadcast_in_dim.101), calls=%async_computation.2 | async-start | bytes 1048576 | tf_op jit(solution)/shard_map/all_to_all | solution.py:53
  41.8 8.5 %all-to-all-start.4 = ((s32[4,1,6]{2,1,0:T(1,128)}), s32[4,1,6]{2,1,0:T(1,128)S(1)}, u32[]{:S(2)}, u32[]{:S(2)}) async-start(s32[4,1,6]{2,1,0:T(1,128)} %broadcast_in_dim.105), calls=%async_computation.4 | async-start | bytes 4096 | tf_op jit(solution)/shard_map/all_to_all | solution.py:53
  58.9 10.5 %copy-start.2 = (u32[256]{0:T(256)S(1)}, u32[256]{0:T(256)}, u32[]{:S(2)}) copy-start(u32[256]{0:T(256)} %constant.64) | copy-start | bytes 3076
  58.9 575.5 %all-to-all-start.3 = ((bf16[64,24,8192]{2,1,0:T(8,128)(2,1)}), bf16[64,24,8192]{2,1,0:T(8,128)(2,1)}, u32[]{:S(2)}, u32[]{:S(2)}) async-start(bf16[64,24,8192]{2,1,0:T(8,128)(2,1)} %stack.3), calls=%async_computation.3 | async-start | bytes 50331648 | tf_op jit(solution)/shard_map/all_to_all | solution.py:17
  709.6 25.6 %copy-start = (f32[6]{0:T(128)}, f32[6]{0:T(128)S(1)}, u32[]{:S(2)}) copy-start(f32[6]{0:T(128)S(1)} %fusion.76) | copy-start | bytes 76
  721.0 14.2 %copy-start.1 = (f32[4]{0:T(128)}, f32[4]{0:T(128)S(1)}, u32[]{:S(2)}) copy-start(f32[4]{0:T(128)S(1)} %reduce_sum.102) | copy-start | bytes 52
